TPU v7x, 32 devices: a whole 2x2x4 slice. The times are simulated.
32 devices in a mesh: group: 8 (over z, y), row: 2 (over x), col: 2 (over core).
Axes of the slice: x: 2, y: 2, z: 4, core: 2. Of those that a mesh axis runs over, the one named last changes fastest.
Arguments:
- tokens: bfloat16 [5120, 2048], P(('group', 'col'), 'row'), may hold values from -6 to 6
- lengths: int32 [24], P('group'), may hold values from 1 to 512, as said below
- norm_gain: float32 [2048], P('row'), may hold values from 0.25 to 1.75
- w_query: bfloat16 [2048, 2048], P('row', 'col'), may hold values from -0.125 to 0.125
- w_key: bfloat16 [2048, 1024], P('row', 'col'), may hold values from -0.125 to 0.125
- w_value: bfloat16 [2048, 1024], P('row', 'col'), may hold values from -0.125 to 0.125
- w_head_gate: bfloat16 [2048, 16], P('row', 'col'), may hold values from -0.25 to 0.25
- query_gain: float32 [128], replicated, may hold values from 1 to 2
- key_gain: float32 [128], replicated, may hold values from 1 to 2
- w_out: bfloat16 [2048, 2048], P('col', 'row'), may hold values from -1.5 to 1.5
- ffn_gain: float32 [2048], P('row'), may hold values from 0.25 to 1.75
- w_gate: bfloat16 [2048, 6144], P('row', 'col'), may hold values from -0.125 to 0.125
- w_up: bfloat16 [2048, 6144], P('row', 'col'), may hold values from -0.125 to 0.125
- w_down: bfloat16 [6144, 2048], P('col', 'row'), may hold values from -0.15625 to 0.15625
- grad_out: bfloat16 [5120, 2048], P(('group', 'col'), 'row'), may hold values from -6 to 6
Outputs:
- output: bfloat16 [5120, 2048], P(('group', 'col'), 'row')
- input_grad: float32 [5120, 2048], P(('group', 'col'), 'row')
- grad_norm_gain: float32 [2048], P('row')
- grad_w_query: float32 [2048, 2048], P('row', 'col')
- grad_w_key: float32 [2048, 1024], P('row', 'col')
- grad_w_value: float32 [2048, 1024], P('row', 'col')
- grad_w_head_gate: float32 [2048, 16], P('row', 'col')
- grad_query_gain: float32 [128], replicated
- grad_key_gain: float32 [128], replicated
- grad_w_out: float32 [2048, 2048], P('col', 'row')
- grad_ffn_gain: float32 [2048], P('row')
- grad_w_gate: float32 [2048, 6144], P('row', 'col')
- grad_w_up: float32 [2048, 6144], P('row', 'col')
- grad_w_down: float32 [6144, 2048], P('col', 'row')
Inputs may be any that keep to these rules, and one draw needn't show every extreme that they name: Each group's 3 entries are the lengths of its sequences in token order; they sum to 640.
All inputs are finite; a program needn't handle non-finite values.
Results may differ from a plain program's by a relative error of at most 0.024.
Values may be sent and summed in bfloat16 or wider, within the bound.
A program may use at most 256 MiB of HBM per device.

v0:
```python
import jax
import jax.numpy as jnp
from jax import lax
from jax.sharding import PartitionSpec as P

EPS = 1e-06
THETA = 1000000.0
NEGATIVE = -1e30


def places(lengths_group, count):
    ends = jnp.cumsum(lengths_group)
    index = jnp.arange(count, dtype=jnp.int32)
    passed = (index[:, None] >= ends[None, :]).astype(jnp.int32)
    segment = jnp.sum(passed, axis=1)
    place = index - jnp.sum(passed * lengths_group[None, :], axis=1)
    return (segment, place)


def rope_tables(place, width):
    half = width // 2
    freq = THETA ** (-(jnp.arange(half, dtype=jnp.float32) * 2.0 / width))
    angle = place.astype(jnp.float32)[:, None] * freq[None, :]
    cosines = jnp.concatenate([jnp.cos(angle), jnp.cos(angle)], axis=1)
    sines = jnp.concatenate([jnp.sin(angle), jnp.sin(angle)], axis=1)
    return (cosines, sines)


def rotate(values, cosines, sines):
    half = values.shape[-1] // 2
    turned = jnp.concatenate([-values[..., half:], values[..., :half]], axis=-1)
    return values * cosines + turned * sines


def unrotate(grads, cosines, sines):
    half = grads.shape[-1] // 2
    scaled = grads * sines
    return grads * cosines + jnp.concatenate([scaled[..., half:], -scaled[..., :half]], axis=-1)


def head_norm_back(d_normed, raw_values, inverse, gain):
    scaled = d_normed * gain
    gain_part = jnp.sum(d_normed * raw_values * inverse, axis=(0, 1))
    d_raw = inverse * scaled - raw_values * inverse**3 * jnp.mean(
        scaled * raw_values, axis=-1, keepdims=True
    )
    return (d_raw, gain_part)


def across_features(values):
    return lax.psum(values, "row")


def gather_tokens(values):
    return lax.all_gather(values, "col", axis=0, tiled=True)


def gather_blocks(values):
    return lax.all_gather(values, "row", axis=0, tiled=True)


def reduce_rows(term, rows):
    return lax.psum_scatter(
        term(jnp.int32(0), lax.axis_size("row") * rows), "row", scatter_dimension=0, tiled=True
    )


def reduce_cols(term, rows):
    return lax.psum_scatter(
        term(jnp.int32(0), lax.axis_size("col") * rows).astype(jnp.bfloat16),
        "col",
        scatter_dimension=0,
        tiled=True,
    ).astype(jnp.float32)


def masked_scores(block_query, block_segment, block_place, key_rows, segment, place, scale):
    scores = (
        jnp.einsum("qkgd,skd->kgqs", block_query, key_rows, preferred_element_type=jnp.float32)
        * scale
    )
    allowed = (block_segment[:, None] == segment[None, :]) & (
        place[None, :] <= block_place[:, None]
    )
    return jnp.where(allowed, scores, NEGATIVE)


def body(
    tokens,
    lengths,
    norm_gain,
    w_query,
    w_key,
    w_value,
    w_head_gate,
    query_gain,
    key_gain,
    w_out,
    ffn_gain,
    w_gate,
    w_up,
    w_down,
    grad_out,
):
    row_count = lax.axis_size("row")
    col_count = lax.axis_size("col")
    tok_dev, d_loc = tokens.shape
    group_tok = tok_dev * col_count
    bin_rows = group_tok // row_count
    head_dim = query_gain.shape[0]
    q_cols = w_query.shape[1]
    kv_cols = w_key.shape[1]
    heads_loc = q_cols // head_dim
    kv_loc = kv_cols // head_dim
    share = heads_loc // kv_loc
    width = d_loc * row_count
    ff_loc = w_gate.shape[1]
    scale = head_dim ** (-0.5)
    blocks = bin_rows // bin_rows
    row_at = lax.axis_index("row")
    position = jnp.arange(group_tok, dtype=jnp.int32)
    order = position % bin_rows * row_count + position // bin_rows
    inverse = position % row_count * bin_rows + position // row_count
    segment, place = places(lengths, group_tok)
    all_segment = segment[order]
    all_place = place[order]
    bin_segment = lax.dynamic_slice_in_dim(all_segment, row_at * bin_rows, bin_rows)
    bin_place = lax.dynamic_slice_in_dim(all_place, row_at * bin_rows, bin_rows)
    x_in = tokens.astype(jnp.float32)
    inverse_one = lax.rsqrt(across_features(jnp.sum(x_in * x_in, axis=1)) / width + EPS)
    normed_one = (x_in * inverse_one[:, None] * norm_gain).astype(jnp.bfloat16)
    gathered_one = gather_tokens(normed_one)
    permuted = gathered_one[order]
    w_first = jnp.concatenate([w_query, w_key, w_value, w_head_gate], axis=1)

    def first_term(start, row_total):
        return jnp.dot(permuted, w_first, preferred_element_type=jnp.float32)

    projected = reduce_rows(first_term, bin_rows)
    raw_query = projected[:, :q_cols].reshape(bin_rows, heads_loc, head_dim)
    raw_key = projected[:, q_cols : q_cols + kv_cols].reshape(bin_rows, kv_loc, head_dim)
    raw_value = projected[:, q_cols + kv_cols : q_cols + 2 * kv_cols].reshape(
        bin_rows, kv_loc, head_dim
    )
    logit = projected[:, q_cols + 2 * kv_cols :]
    query_inverse = lax.rsqrt(jnp.mean(raw_query * raw_query, axis=-1, keepdims=True) + EPS)
    key_inverse = lax.rsqrt(jnp.mean(raw_key * raw_key, axis=-1, keepdims=True) + EPS)
    cosines, sines = rope_tables(bin_place, head_dim)
    cos_heads = cosines[:, None, :]
    sin_heads = sines[:, None, :]
    query = rotate(raw_query * query_inverse * query_gain, cos_heads, sin_heads).astype(
        jnp.bfloat16
    )
    key_local = rotate(raw_key * key_inverse * key_gain, cos_heads, sin_heads).astype(jnp.bfloat16)
    value_local = raw_value.astype(jnp.bfloat16)
    key_rows, value_rows = (
        lax.all_gather(key_local, "row", axis=0, tiled=True),
        lax.all_gather(value_local, "row", axis=0, tiled=True),
    )
    query_blocks = query.reshape(blocks, bin_rows, kv_loc, share, head_dim)
    segment_blocks = bin_segment.reshape(blocks, bin_rows)
    place_blocks = bin_place.reshape(blocks, bin_rows)

    def forward_block(item):
        block_query, block_segment, block_place = item
        scores = masked_scores(
            block_query, block_segment, block_place, key_rows, all_segment, all_place, scale
        )
        top_score = jnp.max(scores, axis=-1, keepdims=True)
        raised = jnp.exp(scores - top_score)
        total = jnp.sum(raised, axis=-1, keepdims=True)
        probs = (raised / total).astype(jnp.bfloat16)
        result = jnp.einsum("kgqs,skd->qkgd", probs, value_rows, preferred_element_type=jnp.float32)
        return (result, top_score[..., 0] + jnp.log(total[..., 0]))

    attended_blocks, logsum_blocks = lax.map(
        forward_block, (query_blocks, segment_blocks, place_blocks)
    )
    attended = attended_blocks.reshape(bin_rows, heads_loc, head_dim)
    gate_sigmoid = jax.nn.sigmoid(logit)
    gated = (attended * gate_sigmoid[:, :, None]).reshape(bin_rows, q_cols).astype(jnp.bfloat16)
    gathered_gated = gather_blocks(gated)

    def out_term(start, row_total):
        return jnp.dot(gathered_gated[inverse], w_out, preferred_element_type=jnp.float32)

    attn_branch = reduce_cols(out_term, tok_dev)
    resid = x_in + attn_branch
    inverse_two = lax.rsqrt(across_features(jnp.sum(resid * resid, axis=1)) / width + EPS)
    normed_two = (resid * inverse_two[:, None] * ffn_gain).astype(jnp.bfloat16)
    gathered_two = gather_tokens(normed_two)
    w_pair = jnp.concatenate([w_gate, w_up], axis=1)
    pair_value = lax.psum_scatter(
        jnp.dot(gathered_two, w_pair, preferred_element_type=jnp.float32).astype(jnp.bfloat16),
        "row",
        scatter_dimension=0,
        tiled=True,
    ).astype(jnp.float32)
    gate_part = pair_value[:, :ff_loc]
    up_part = pair_value[:, ff_loc:]
    gate_sig = jax.nn.sigmoid(gate_part)
    silu_part = gate_part * gate_sig
    inner = (silu_part * up_part).astype(jnp.bfloat16)
    gathered_inner = gather_blocks(inner)

    def down_term(start, row_total):
        return jnp.dot(gathered_inner, w_down, preferred_element_type=jnp.float32)

    branch = reduce_cols(down_term, tok_dev)
    output = (resid + branch).astype(jnp.bfloat16)
    d_top = grad_out.astype(jnp.float32)
    gathered_grad = gather_tokens(grad_out)
    grad_down = jnp.einsum(
        "tf,td->fd", gathered_inner, gathered_grad, preferred_element_type=jnp.float32
    )

    def inner_term(start, row_total):
        return jnp.einsum("td,fd->tf", gathered_grad, w_down, preferred_element_type=jnp.float32)

    d_inner = reduce_rows(inner_term, bin_rows)
    d_gate = d_inner * up_part * (gate_sig * (1.0 + gate_part * (1.0 - gate_sig)))
    d_up = d_inner * silu_part
    d_pair = jnp.concatenate([d_gate, d_up], axis=1).astype(jnp.bfloat16)
    gathered_pair = lax.all_gather(d_pair, "row", axis=0, tiled=True)
    whole_grad = jnp.einsum(
        "td,tf->df", gathered_two, gathered_pair, preferred_element_type=jnp.float32
    )
    grad_gate = whole_grad[:, :ff_loc]
    grad_up = whole_grad[:, ff_loc:]

    def norm_term(start, row_total):
        return jnp.einsum("tf,df->td", gathered_pair, w_pair, preferred_element_type=jnp.float32)

    d_normed_two = reduce_cols(norm_term, tok_dev)
    ffn_gain_part = jnp.sum(d_normed_two * resid * inverse_two[:, None], axis=0)
    scaled_two = d_normed_two * ffn_gain
    inner_two = across_features(jnp.sum(scaled_two * resid, axis=1))
    d_resid = (
        d_top
        + inverse_two[:, None] * scaled_two
        - resid * (inverse_two**3 * inner_two / width)[:, None]
    )
    d_branch = d_resid.astype(jnp.bfloat16)
    gathered_branch = gather_tokens(d_branch)
    permuted_branch = gathered_branch[order]
    grad_out_w = jnp.einsum(
        "tq,td->qd", gathered_gated, permuted_branch, preferred_element_type=jnp.float32
    )

    def gated_term(start, row_total):
        return jnp.einsum("td,qd->tq", permuted_branch, w_out, preferred_element_type=jnp.float32)

    d_gated = reduce_rows(gated_term, bin_rows).reshape(bin_rows, heads_loc, head_dim)
    d_attended = (d_gated * gate_sigmoid[:, :, None]).astype(jnp.bfloat16)
    d_logit = jnp.sum(d_gated * attended, axis=-1) * gate_sigmoid * (1.0 - gate_sigmoid)
    d_attended_blocks = d_attended.reshape(blocks, bin_rows, kv_loc, share, head_dim)

    def backward_block(carry, item):
        d_key_sum, d_value_sum = carry
        block_query, block_segment, block_place, block_grad, block_logsum = item
        scores = masked_scores(
            block_query, block_segment, block_place, key_rows, all_segment, all_place, scale
        )
        probs = jnp.exp(scores - block_logsum[..., None])
        d_probs = jnp.einsum(
            "qkgd,skd->kgqs", block_grad, value_rows, preferred_element_type=jnp.float32
        )
        d_scores = (probs * (d_probs - jnp.sum(d_probs * probs, axis=-1, keepdims=True))).astype(
            jnp.bfloat16
        )
        d_query_block = (
            jnp.einsum("kgqs,skd->qkgd", d_scores, key_rows, preferred_element_type=jnp.float32)
            * scale
        )
        d_key_sum = (
            d_key_sum
            + jnp.einsum(
                "kgqs,qkgd->skd", d_scores, block_query, preferred_element_type=jnp.float32
            )
            * scale
        )
        d_value_sum = d_value_sum + jnp.einsum(
            "kgqs,qkgd->skd",
            probs.astype(jnp.bfloat16),
            block_grad,
            preferred_element_type=jnp.float32,
        )
        return ((d_key_sum, d_value_sum), d_query_block)

    zero_rows = jnp.zeros((group_tok, kv_loc, head_dim), jnp.float32)
    (d_key_all, d_value_all), d_query_blocks = lax.scan(
        backward_block,
        (zero_rows, zero_rows),
        (query_blocks, segment_blocks, place_blocks, d_attended_blocks, logsum_blocks),
    )
    d_keys, d_values = (
        lax.psum_scatter(
            d_key_all.astype(jnp.bfloat16), "row", scatter_dimension=0, tiled=True
        ).astype(jnp.float32),
        lax.psum_scatter(
            d_value_all.astype(jnp.bfloat16), "row", scatter_dimension=0, tiled=True
        ).astype(jnp.float32),
    )
    d_query = d_query_blocks.reshape(bin_rows, heads_loc, head_dim)
    d_raw_query, query_gain_part = head_norm_back(
        unrotate(d_query, cos_heads, sin_heads), raw_query, query_inverse, query_gain
    )
    d_raw_key, key_gain_part = head_norm_back(
        unrotate(d_keys, cos_heads, sin_heads), raw_key, key_inverse, key_gain
    )
    d_projected = jnp.concatenate(
        [
            d_raw_query.reshape(bin_rows, q_cols),
            d_raw_key.reshape(bin_rows, kv_cols),
            d_values.reshape(bin_rows, kv_cols),
            d_logit,
        ],
        axis=1,
    ).astype(jnp.bfloat16)
    gathered_first = gather_blocks(d_projected)
    grad_first = jnp.einsum(
        "td,tc->dc", permuted, gathered_first, preferred_element_type=jnp.float32
    )

    def first_back_term(start, row_total):
        return jnp.einsum(
            "tc,dc->td", gathered_first[inverse], w_first, preferred_element_type=jnp.float32
        )

    d_normed_one = reduce_cols(first_back_term, tok_dev)
    norm_gain_part = jnp.sum(d_normed_one * x_in * inverse_one[:, None], axis=0)
    scaled_one = d_normed_one * norm_gain
    inner_one = across_features(jnp.sum(scaled_one * x_in, axis=1))
    input_grad = (
        d_resid
        + inverse_one[:, None] * scaled_one
        - x_in * (inverse_one**3 * inner_one / width)[:, None]
    )
    grad_norm_gain, grad_ffn_gain = lax.psum((norm_gain_part, ffn_gain_part), ("group", "col"))
    grad_query_gain, grad_key_gain = lax.psum(
        (query_gain_part, key_gain_part), ("group", "row", "col")
    )
    grad_query = grad_first[:, :q_cols]
    grad_key = grad_first[:, q_cols : q_cols + kv_cols]
    grad_value = grad_first[:, q_cols + kv_cols : q_cols + 2 * kv_cols]
    grad_head_gate = grad_first[:, q_cols + 2 * kv_cols :]
    summed = (
        lax.psum(grad_query.astype(jnp.bfloat16), "group").astype(jnp.float32),
        lax.psum(grad_key.astype(jnp.bfloat16), "group").astype(jnp.float32),
        lax.psum(grad_value.astype(jnp.bfloat16), "group").astype(jnp.float32),
        lax.psum(grad_head_gate.astype(jnp.bfloat16), "group").astype(jnp.float32),
        lax.psum(grad_out_w.astype(jnp.bfloat16), "group").astype(jnp.float32),
        lax.psum(grad_gate.astype(jnp.bfloat16), "group").astype(jnp.float32),
        lax.psum(grad_up.astype(jnp.bfloat16), "group").astype(jnp.float32),
        lax.psum(grad_down.astype(jnp.bfloat16), "group").astype(jnp.float32),
    )
    return (
        output,
        input_grad,
        grad_norm_gain,
        summed[0],
        summed[1],
        summed[2],
        summed[3],
        grad_query_gain,
        grad_key_gain,
        summed[4],
        grad_ffn_gain,
        summed[5],
        summed[6],
        summed[7],
    )


def solution(mesh):
    in_specs = (
        P(("group", "col"), "row"),
        P("group"),
        P("row"),
        P("row", "col"),
        P("row", "col"),
        P("row", "col"),
        P("row", "col"),
        P(),
        P(),
        P("col", "row"),
        P("row"),
        P("row", "col"),
        P("row", "col"),
        P("col", "row"),
        P(("group", "col"), "row"),
    )
    out_specs = (
        P(("group", "col"), "row"),
        P(("group", "col"), "row"),
        P("row"),
        P("row", "col"),
        P("row", "col"),
        P("row", "col"),
        P("row", "col"),
        P(),
        P(),
        P("col", "row"),
        P("row"),
        P("row", "col"),
        P("row", "col"),
        P("col", "row"),
    )
    return jax.shard_map(body, mesh=mesh, in_specs=in_specs, out_specs=out_specs, check_vma=False)
```

profile of v0, /device:TPU:0, one launch (start us, length us, event | category | flops | bytes accessed | tf_op | source)
XLA Modules:
  0.0 1673.6 jit_solution(9687963277787072502)
XLA Ops:
  18.3 10.4 all-gather.9.cloned.1.call-done
  52.2 60.9 %reduce-scatter.28.cloned.1.call-done = f32[320,2056]{1,0:T(8,128)} async-done(((f32[640,2056]{1,0:T(8,128)}), f32[320,2056]{1,0:T(8,128)}) %reduce-scatter.28.cloned.1.call-update) | async-done | bytes 2631696 | tf_op jit(solution)/shard_map/reduce_scatter | solution.py:63
  134.4 10.9 all_gather.31
  149.0 10.0 all_gather.32
  185.8 25.1 %all-gather.11.cloned.1.call-done = bf16[640,1024]{1,0:T(8,128)(2,1)} async-done(((bf16[320,1024]{1,0:T(8,128)(2,1)}), bf16[640,1024]{1,0:T(8,128)(2,1)}) %all-gather.11.cloned.1.call-update) | async-done | bytes 1310736 | tf_op jit(solution)/shard_map/all_gather | solution.py:59
  251.4 15.2 convolution_convert_fusion.1
  266.7 10.7 fusion.84
  277.4 84.6 %reduce-scatter.14.cloned.1.call-done = bf16[320,6144]{1,0:T(8,128)(2,1)} async-done(((bf16[640,6144]{1,0:T(8,128)(2,1)}), bf16[320,6144]{1,0:T(8,128)(2,1)}) %reduce-scatter.14.cloned.1.call-update) | async-done | bytes 3932176 | tf_op jit(solution)/shard_map/reduce_scatter | solution.py:193
  368.3 90.8 %reduce-scatter.18.cloned.1.call-done = f32[320,3072]{1,0:T(8,128)} async-done(((f32[640,3072]{1,0:T(8,128)}), f32[320,3072]{1,0:T(8,128)}) %reduce-scatter.18.cloned.1.call-update) | async-done | bytes 3932176 | tf_op jit(solution)/shard_map/reduce_scatter | solution.py:63
  468.5 97.8 %all-gather.19.cloned.1.call-done = bf16[640,6144]{1,0:T(8,128)(2,1)} async-done(((bf16[320,6144]{1,0:T(8,128)(2,1)}), bf16[640,6144]{1,0:T(8,128)(2,1)}) %all-gather.19.cloned.1.call-update) | async-done | bytes 7864336 | tf_op jit(solution)/shard_map/all_gather | solution.py:224
  566.3 14.4 convolution_convert_fusion.6
  599.3 10.7 all-gather.21.cloned.1.call-done
  626.7 32.6 %reduce-scatter.22.cloned.1.call-done = f32[320,1024]{1,0:T(8,128)} async-done(((f32[640,1024]{1,0:T(8,128)}), f32[320,1024]{1,0:T(8,128)}) %reduce-scatter.22.cloned.1.call-update) | async-done | bytes 1310736 | tf_op jit(solution)/shard_map/reduce_scatter | solution.py:63
  711.1 12.1 reduce-scatter.24.cloned.1.call-done
  728.9 40.4 %all-gather.23.cloned.1.call-done = bf16[640,2056]{1,0:T(8,128)(2,1)} async-done(((bf16[320,2056]{1,0:T(8,128)(2,1)}), bf16[640,2056]{1,0:T(8,128)(2,1)}) %all-gather.23.cloned.1.call-update) | async-done | bytes 2631696 | tf_op jit(solution)/shard_map/all_gather | solution.py:59
  769.3 9.3 gather_fusion.5
  786.4 38.8 %all-gather.15.cloned.1.call-done = bf16[640,3072]{1,0:T(8,128)(2,1)} async-done(((bf16[320,3072]{1,0:T(8,128)(2,1)}), bf16[640,3072]{1,0:T(8,128)(2,1)}) %all-gather.15.cloned.1.call-update) | async-done | bytes 3932176 | tf_op jit(solution)/shard_map/all_gather | solution.py:59
  834.9 9.5 convolution_convert_fusion.2
  844.5 14.4 convolution_convert_fusion
  875.1 44.0 %all-reduce.1 = (f32[128]{0:T(128)}, f32[128]{0:T(128)}) all-reduce(f32[128]{0:T(128)S(1)} %bitcast_reduce_fusion, f32[128]{0:T(128)S(1)} %get-tuple-element.197), channel_id=1, replica_groups=mesh['group'=8,'row'=2,'col'=2] {'group','row','col'}, use_global_device_ids=true, to_apply=%region_37.38 | all-reduce | flops 256 | bytes 2048 | tf_op jit(solution)/shard_map/psum | solution.py:340
  919.1 37.7 %psum.120 = bf16[1024,8]{0,1:T(8,128)(2,1)S(1)} all-reduce(bf16[1024,8]{0,1:T(8,128)(2,1)S(1)} %slice-done.6), channel_id=1, replica_groups=mesh['group'=8,'row'=2,'col'=2] {'group'}, use_global_device_ids=true, to_apply=%region_34.35 | all-reduce | flops 8192 | bytes 32768 | tf_op jit(solution)/shard_map/psum | solution.py:351
  964.0 34.1 %all-reduce.2 = (f32[1024]{0:T(1024)}, f32[1024]{0:T(1024)}) all-reduce(f32[1024]{0:T(1024)S(1)} %get-tuple-element.199, f32[1024]{0:T(1024)S(1)} %get-tuple-element.195), channel_id=1, replica_groups=mesh['group'=8,'row'=2,'col'=2] {'group','col'}, use_global_device_ids=true, to_apply=%region_30.31 | all-reduce | flops 2048 | bytes 16384 | tf_op jit(solution)/shard_map/psum | solution.py:339
  1001.6 632.3 %all-reduce.9.cloned.1.call-done = (bf16[1024,1024]{0,1:T(8,128)(2,1)}, bf16[1024,512]{0,1:T(8,128)(2,1)}, bf16[1024,512]{0,1:T(8,128)(2,1)}, bf16[1024,1024]{1,...) async-done(((bf16[1024,1024]{0,1:T(8,128)(2,1)}, bf16[1024,512]{0,1:T(8,128)(2,1)}, ...) | async-done | bytes 25165840 | tf_op jit(solution)/shard_map/psum | solution.py:348
  1644.7 9.4 convert_element_type.179
  (321 shorter events, 301.9 us)
Async XLA Ops:
  7.2 209.6 %copy-start = (bf16[1024,1024]{1,0:T(8,128)(2,1)S(1)}, bf16[1024,1024]{1,0:T(8,128)(2,1)}, u32[]{:S(2)}) copy-start(bf16[1024,1024]{1,0:T(8,128)(2,1)} %param.24) | copy-start | bytes 6291460
  7.2 21.5 %all-gather.9.cloned.1.call-start = ((), (), s32[]{:S(2)}) async-start(), calls=%async_computation.9 | async-start | bytes 1966080 | tf_op jit(solution)/shard_map/all_gather | solution.py:55
  17.3 95.9 %reduce-scatter.28.cloned.1.call-start = ((), (), s32[]{:S(2)}) async-start(), calls=%async_computation.25 | async-start | bytes 8355840 | tf_op jit(solution)/shard_map/reduce_scatter | solution.py:63
  42.6 168.3 %all-gather.11.cloned.1.call-start = ((), (), s32[]{:S(2)}) async-start(), calls=%async_computation.10 | async-start | bytes 1966080 | tf_op jit(solution)/shard_map/all_gather | solution.py:59
  185.7 43.9 %reduce-scatter.12.cloned.1.call-start = ((), (), s32[]{:S(2)}) async-start(), calls=%async_computation.11 | async-start | bytes 1966080 | tf_op jit(solution)/shard_map/reduce_scatter | solution.py:69
  220.7 30.7 %all-gather.13.cloned.1.call-start = ((), (), s32[]{:S(2)}) async-start(), calls=%async_computation.12 | async-start | bytes 1966080 | tf_op jit(solution)/shard_map/all_gather | solution.py:55
  238.2 28.5 %all-gather.17.cloned.1.call-start = ((), (), s32[]{:S(2)}) async-start(), calls=%async_computation.16 | async-start | bytes 1966080 | tf_op jit(solution)/shard_map/all_gather | solution.py:55
  238.8 123.3 %reduce-scatter.14.cloned.1.call-start = ((), (), s32[]{:S(2)}) async-start(), calls=%async_computation.13 | async-start | bytes 11796480 | tf_op jit(solution)/shard_map/reduce_scatter | solution.py:193
  266.6 192.5 %reduce-scatter.18.cloned.1.call-start = ((), (), s32[]{:S(2)}) async-start(), calls=%async_computation.17 | async-start | bytes 11796480 | tf_op jit(solution)/shard_map/reduce_scatter | solution.py:63
  277.4 288.9 %all-gather.19.cloned.1.call-start = ((), (), s32[]{:S(2)}) async-start(), calls=%async_computation.18 | async-start | bytes 11796480 | tf_op jit(solution)/shard_map/all_gather | solution.py:224
  468.0 121.6 %reduce-scatter.20.cloned.1.call-start = ((), (), s32[]{:S(2)}) async-start(), calls=%async_computation.19 | async-start | bytes 1966080 | tf_op jit(solution)/shard_map/reduce_scatter | solution.py:69
  580.7 29.3 %all-gather.21.cloned.1.call-start = ((), (), s32[]{:S(2)}) async-start(), calls=%async_computation.20 | async-start | bytes 1966080 | tf_op jit(solution)/shard_map/all_gather | solution.py:55
  599.2 60.0 %reduce-scatter.22.cloned.1.call-start = ((), (), s32[]{:S(2)}) async-start(), calls=%async_computation.21 | async-start | bytes 3932160 | tf_op jit(solution)/shard_map/reduce_scatter | solution.py:63
  620.3 88.9 %all-reduce.7.cloned.1.call-start = ((), (), s32[]{:S(2)}) async-start(), calls=%async_computation.26 | async-start | bytes 1310720
  672.8 50.3 %reduce-scatter.24.cloned.1.call-start = ((), (), s32[]{:S(2)}) async-start(), calls=%async_computation.22 | async-start | bytes 983040 | tf_op jit(solution)/shard_map/reduce_scatter | solution.py:297
  695.8 73.5 %all-gather.23.cloned.1.call-start = ((), (), s32[]{:S(2)}) async-start(), calls=%async_computation.23 | async-start | bytes 4177920 | tf_op jit(solution)/shard_map/all_gather | solution.py:59
  728.3 96.9 %all-gather.15.cloned.1.call-start = ((), (), s32[]{:S(2)}) async-start(), calls=%async_computation.14 | async-start | bytes 5898240 | tf_op jit(solution)/shard_map/all_gather | solution.py:59
  728.9 228.6 %reduce-scatter.26.cloned.1.call-start = ((), (), s32[]{:S(2)}) async-start(), calls=%async_computation.24 | async-start | bytes 1966080 | tf_op jit(solution)/shard_map/reduce_scatter | solution.py:69
  786.3 211.8 %reduce-scatter.16.cloned.1.call-start = ((), (), s32[]{:S(2)}) async-start(), calls=%async_computation.15 | async-start | bytes 1966080 | tf_op jit(solution)/shard_map/reduce_scatter | solution.py:69
  834.5 799.4 %all-reduce.9.cloned.1.call-start = ((), (), s32[]{:S(2)}) async-start(), calls=%async_computation.27 | async-start | bytes 50331648 | tf_op jit(solution)/shard_map/psum | solution.py:348
  875.0 123.0 %copy-start.56 = (f32[320]{0:T(512)S(1)}, f32[320]{0:T(512)}, u32[]{:S(2)}) copy-start(f32[320]{0:T(512)} %copy-done.55) | copy-start | bytes 3844
  875.0 123.1 %copy-start.18 = (bf16[320,1024]{1,0:T(8,128)(2,1)S(1)}, bf16[320,1024]{1,0:T(8,128)(2,1)}, u32[]{:S(2)}) copy-start(bf16[320,1024]{1,0:T(8,128)(2,1)} %reduce-scatter.20.cloned.1.call-done) | copy-start | bytes 1966084
  875.1 123.0 %copy-start.10 = (bf16[320,1024]{1,0:T(8,128)(2,1)S(1)}, bf16[320,1024]{1,0:T(8,128)(2,1)}, u32[]{:S(2)}) copy-start(bf16[320,1024]{1,0:T(8,128)(2,1)} %reduce-scatter.12.cloned.1.call-done) | copy-start | bytes 1966084
  875.1 123.0 %copy-start.17 = (bf16[320,1024]{1,0:T(8,128)(2,1)S(1)}, bf16[320,1024]{1,0:T(8,128)(2,1)}, u32[]{:S(2)}) copy-start(bf16[320,1024]{1,0:T(8,128)(2,1)} %param.29) | copy-start | bytes 1966084
  (66 other events, 604.1 us)
Sparse Core Ops, SparseCore 0:
  17.4 11.2 all-gather.8
  42.7 70.4 reduce-scatter.27
  185.8 24.9 all-gather.10
  220.9 8.7 reduce-scatter.11
  238.3 10.6 all-gather.12
  250.5 10.5 all-gather.16
  266.7 95.2 reduce-scatter.13
  364.9 94.1 reduce-scatter.17
  468.1 98.0 all-gather.18
  580.8 8.7 reduce-scatter.19
  599.4 10.5 all-gather.20
  620.4 38.7 reduce-scatter.21
  673.0 31.4 all-reduce.6
  707.1 15.9 reduce-scatter.23
  728.4 40.8 all-gather.22
  771.4 53.7 all-gather.14
  827.9 8.7 reduce-scatter.25
  839.4 9.9 reduce-scatter.15
  875.2 758.6 all-reduce.8
where the time goes:
time: 1680 us; the launch traced here: 1670 us
  waiting for transfers between devices  1160 us (69%)
  blocking collectives  157 us (9%)
  local copies, waits for them, and re-layouts  131 us (8%)
  matrix products  123 us (7%)
  other arithmetic  88.9 us (5%)
    psum x1, waiting for transfers between devices, body(): lax.psum(grad_query.astype(jnp.bfloat16), 'group').astype(jnp.float32)  632 us
    reduce_scatter x3, waiting for transfers between devices, reduce_rows(): lax.psum_scatter(term(jnp.int32(0), lax.axis_size('row') * rows), 'row',...  184 us
    all_gather x3, waiting for transfers between devices, gather_blocks(): return lax.all_gather(values, 'row', axis=0, tiled=True)  104 us
    all_gather x1, waiting for transfers between devices, body(): gathered_pair = lax.all_gather(d_pair, 'row', axis=0, tiled=True)  97.8 us
    reduce_scatter x1, waiting for transfers between devices, body(): lax.psum_scatter(jnp.dot(gathered_two, w_pair, preferred_element_type=jnp...  84.6 us
    psum x1, blocking collectives, body(): lax.psum((query_gain_part, key_gain_part), ('group', 'row', 'col'))  44 us
    psum x1, blocking collectives, body(): lax.psum(grad_head_gate.astype(jnp.bfloat16), 'group').astype(jnp.float32)  37.7 us
    psum x1, blocking collectives, body(): lax.psum((norm_gain_part, ffn_gain_part), ('group', 'col'))  34.1 us
  transfers between devices with their start and end apart: 19, of which 14 were waited for; matrix products, arithmetic and copies ran while one was open for 10% of the time, Pallas kernels for 0%

commit v1 on v0

--- a/solution.py
+++ b/solution.py
@@ -348,7 +348,9 @@
         lax.psum(grad_query.astype(jnp.bfloat16), "group").astype(jnp.float32),
         lax.psum(grad_key.astype(jnp.bfloat16), "group").astype(jnp.float32),
         lax.psum(grad_value.astype(jnp.bfloat16), "group").astype(jnp.float32),
-        lax.psum(grad_head_gate.astype(jnp.bfloat16), "group").astype(jnp.float32),
+        jnp.sum(lax.all_gather(grad_head_gate.astype(jnp.bfloat16), "group"), axis=0).astype(
+            jnp.float32
+        ),
         lax.psum(grad_out_w.astype(jnp.bfloat16), "group").astype(jnp.float32),
         lax.psum(grad_gate.astype(jnp.bfloat16), "group").astype(jnp.float32),
         lax.psum(grad_up.astype(jnp.bfloat16), "group").astype(jnp.float32),

time: 1680 us -> 1680 us (level)
    psum x1 -> x0, blocking collectives: 37.7 us -> none  [body(): lax.psum(grad_head_gate.astype(jnp.bfloat16), 'group').astype(jnp.float32)]
    all_gather x0 -> x1, blocking collectives: none -> 32.4 us  [body(): lax.all_gather(grad_head_gate.astype(jnp.bfloat16), 'group')]
where the time goes in v1:
time: 1680 us; the launch traced here: 1670 us
  waiting for transfers between devices  1160 us (69%)
  blocking collectives  152 us (9%)
  local copies, waits for them, and re-layouts  131 us (8%)
  matrix products  123 us (7%)
  other arithmetic  89 us (5%)
    psum x1, waiting for transfers between devices, body(): lax.psum(grad_query.astype(jnp.bfloat16), 'group').astype(jnp.float32)  638 us
    reduce_scatter x3, waiting for transfers between devices, reduce_rows(): lax.psum_scatter(term(jnp.int32(0), lax.axis_size('row') * rows), 'row',...  184 us
    all_gather x3, waiting for transfers between devices, gather_blocks(): return lax.all_gather(values, 'row', axis=0, tiled=True)  104 us
    all_gather x1, waiting for transfers between devices, body(): gathered_pair = lax.all_gather(d_pair, 'row', axis=0, tiled=True)  97.8 us
    reduce_scatter x1, waiting for transfers between devices, body(): lax.psum_scatter(jnp.dot(gathered_two, w_pair, preferred_element_type=jnp...  84.6 us
    psum x1, blocking collectives, body(): lax.psum((query_gain_part, key_gain_part), ('group', 'row', 'col'))  43.8 us
    psum x1, blocking collectives, body(): lax.psum((norm_gain_part, ffn_gain_part), ('group', 'col'))  34 us
    unnamed x147, local copies, waits for them, and re-layouts  33.7 us
  transfers between devices with their start and end apart: 19, of which 14 were waited for; matrix products, arithmetic and copies ran while one was open for 10% of the time, Pallas kernels for 0%

profile of v1, /device:TPU:0, one launch (start us, length us, event | category | flops | bytes accessed | tf_op | source)
XLA Modules:
  0.0 1673.5 jit_solution(17470660931360968400)
XLA Ops:
  18.3 10.4 all-gather.10.cloned.1.call-done
  52.2 60.9 %reduce-scatter.28.cloned.1.call-done = f32[320,2056]{1,0:T(8,128)} async-done(((f32[640,2056]{1,0:T(8,128)}), f32[320,2056]{1,0:T(8,128)}) %reduce-scatter.28.cloned.1.call-update) | async-done | bytes 2631696 | tf_op jit(solution)/shard_map/reduce_scatter | solution.py:63
  134.4 10.9 all_gather.37
  149.0 10.0 all_gather.38
  185.8 25.1 %all-gather.12.cloned.1.call-done = bf16[640,1024]{1,0:T(8,128)(2,1)} async-done(((bf16[320,1024]{1,0:T(8,128)(2,1)}), bf16[640,1024]{1,0:T(8,128)(2,1)}) %all-gather.12.cloned.1.call-update) | async-done | bytes 1310736 | tf_op jit(solution)/shard_map/all_gather | solution.py:59
  251.4 15.2 convolution_convert_fusion.1
  266.7 10.7 fusion.84
  277.4 84.6 %reduce-scatter.14.cloned.1.call-done = bf16[320,6144]{1,0:T(8,128)(2,1)} async-done(((bf16[640,6144]{1,0:T(8,128)(2,1)}), bf16[320,6144]{1,0:T(8,128)(2,1)}) %reduce-scatter.14.cloned.1.call-update) | async-done | bytes 3932176 | tf_op jit(solution)/shard_map/reduce_scatter | solution.py:193
  368.3 90.8 %reduce-scatter.18.cloned.1.call-done = f32[320,3072]{1,0:T(8,128)} async-done(((f32[640,3072]{1,0:T(8,128)}), f32[320,3072]{1,0:T(8,128)}) %reduce-scatter.18.cloned.1.call-update) | async-done | bytes 3932176 | tf_op jit(solution)/shard_map/reduce_scatter | solution.py:63
  468.5 97.8 %all-gather.20.cloned.1.call-done = bf16[640,6144]{1,0:T(8,128)(2,1)} async-done(((bf16[320,6144]{1,0:T(8,128)(2,1)}), bf16[640,6144]{1,0:T(8,128)(2,1)}) %all-gather.20.cloned.1.call-update) | async-done | bytes 7864336 | tf_op jit(solution)/shard_map/all_gather | solution.py:224
  566.3 14.4 convolution_convert_fusion.6
  599.3 10.7 all-gather.22.cloned.1.call-done
  626.7 32.6 %reduce-scatter.22.cloned.1.call-done = f32[320,1024]{1,0:T(8,128)} async-done(((f32[640,1024]{1,0:T(8,128)}), f32[320,1024]{1,0:T(8,128)}) %reduce-scatter.22.cloned.1.call-update) | async-done | bytes 1310736 | tf_op jit(solution)/shard_map/reduce_scatter | solution.py:63
  711.1 12.1 reduce-scatter.24.cloned.1.call-done
  728.9 40.4 %all-gather.24.cloned.1.call-done = bf16[640,2056]{1,0:T(8,128)(2,1)} async-done(((bf16[320,2056]{1,0:T(8,128)(2,1)}), bf16[640,2056]{1,0:T(8,128)(2,1)}) %all-gather.24.cloned.1.call-update) | async-done | bytes 2631696 | tf_op jit(solution)/shard_map/all_gather | solution.py:59
  769.3 9.3 gather_fusion.5
  786.8 38.4 %all-gather.16.cloned.1.call-done = bf16[640,3072]{1,0:T(8,128)(2,1)} async-done(((bf16[320,3072]{1,0:T(8,128)(2,1)}), bf16[640,3072]{1,0:T(8,128)(2,1)}) %all-gather.16.cloned.1.call-update) | async-done | bytes 3932176 | tf_op jit(solution)/shard_map/all_gather | solution.py:59
  834.5 9.6 convolution_convert_fusion.2
  844.1 14.4 convolution_convert_fusion
  874.8 43.8 %all-reduce.1 = (f32[128]{0:T(128)}, f32[128]{0:T(128)}) all-reduce(f32[128]{0:T(128)S(1)} %bitcast_reduce_fusion, f32[128]{0:T(128)S(1)} %get-tuple-element.197), channel_id=1, replica_groups=mesh['group'=8,'row'=2,'col'=2] {'group','row','col'}, use_global_device_ids=true, to_apply=%region_37.38 | all-reduce | flops 256 | bytes 2048 | tf_op jit(solution)/shard_map/psum | solution.py:340
  918.6 32.4 %all-gather = bf16[8192,8]{0,1:T(8,128)(2,1)S(1)} all-gather(bf16[1024,8]{0,1:T(8,128)(2,1)S(1)} %slice-done.6), channel_id=2, replica_groups=mesh['group'=8,'row'=2,'col'=2] {'group'}, dimensions={0}, use_global_device_ids=true | all-gather | bytes 147456 | tf_op jit(solution)/shard_map/all_gather | solution.py:351
  958.1 34.0 %all-reduce.2 = (f32[1024]{0:T(1024)}, f32[1024]{0:T(1024)}) all-reduce(f32[1024]{0:T(1024)S(1)} %get-tuple-element.199, f32[1024]{0:T(1024)S(1)} %get-tuple-element.195), channel_id=1, replica_groups=mesh['group'=8,'row'=2,'col'=2] {'group','col'}, use_global_device_ids=true, to_apply=%region_30.31 | all-reduce | flops 2048 | bytes 16384 | tf_op jit(solution)/shard_map/psum | solution.py:339
  995.7 638.1 %all-reduce.9.cloned.1.call-done = (bf16[1024,1024]{0,1:T(8,128)(2,1)}, bf16[1024,512]{0,1:T(8,128)(2,1)}, bf16[1024,512]{0,1:T(8,128)(2,1)}, bf16[1024,1024]{1,...) async-done(((bf16[1024,1024]{0,1:T(8,128)(2,1)}, bf16[1024,512]{0,1:T(8,128)(2,1)}, ...) | async-done | bytes 25165840 | tf_op jit(solution)/shard_map/psum | solution.py:348
  1644.6 9.4 convert_element_type.181
  (322 shorter events, 302.0 us)
Async XLA Ops:
  7.2 209.6 %copy-start = (bf16[1024,1024]{1,0:T(8,128)(2,1)S(1)}, bf16[1024,1024]{1,0:T(8,128)(2,1)}, u32[]{:S(2)}) copy-start(bf16[1024,1024]{1,0:T(8,128)(2,1)} %param.24) | copy-start | bytes 6291460
  7.2 21.5 %all-gather.10.cloned.1.call-start = ((), (), s32[]{:S(2)}) async-start(), calls=%async_computation.9 | async-start | bytes 1966080 | tf_op jit(solution)/shard_map/all_gather | solution.py:55
  17.3 95.9 %reduce-scatter.28.cloned.1.call-start = ((), (), s32[]{:S(2)}) async-start(), calls=%async_computation.25 | async-start | bytes 8355840 | tf_op jit(solution)/shard_map/reduce_scatter | solution.py:63
  42.6 168.3 %all-gather.12.cloned.1.call-start = ((), (), s32[]{:S(2)}) async-start(), calls=%async_computation.10 | async-start | bytes 1966080 | tf_op jit(solution)/shard_map/all_gather | solution.py:59
  185.7 43.9 %reduce-scatter.12.cloned.1.call-start = ((), (), s32[]{:S(2)}) async-start(), calls=%async_computation.11 | async-start | bytes 1966080 | tf_op jit(solution)/shard_map/reduce_scatter | solution.py:69
  220.7 30.7 %all-gather.14.cloned.1.call-start = ((), (), s32[]{:S(2)}) async-start(), calls=%async_computation.12 | async-start | bytes 1966080 | tf_op jit(solution)/shard_map/all_gather | solution.py:55
  238.2 28.5 %all-gather.18.cloned.1.call-start = ((), (), s32[]{:S(2)}) async-start(), calls=%async_computation.16 | async-start | bytes 1966080 | tf_op jit(solution)/shard_map/all_gather | solution.py:55
  238.8 123.3 %reduce-scatter.14.cloned.1.call-start = ((), (), s32[]{:S(2)}) async-start(), calls=%async_computation.13 | async-start | bytes 11796480 | tf_op jit(solution)/shard_map/reduce_scatter | solution.py:193
  266.6 192.5 %reduce-scatter.18.cloned.1.call-start = ((), (), s32[]{:S(2)}) async-start(), calls=%async_computation.17 | async-start | bytes 11796480 | tf_op jit(solution)/shard_map/reduce_scatter | solution.py:63
  277.4 288.9 %all-gather.20.cloned.1.call-start = ((), (), s32[]{:S(2)}) async-start(), calls=%async_computation.18 | async-start | bytes 11796480 | tf_op jit(solution)/shard_map/all_gather | solution.py:224
  468.0 121.6 %reduce-scatter.20.cloned.1.call-start = ((), (), s32[]{:S(2)}) async-start(), calls=%async_computation.19 | async-start | bytes 1966080 | tf_op jit(solution)/shard_map/reduce_scatter | solution.py:69
  580.7 29.3 %all-gather.22.cloned.1.call-start = ((), (), s32[]{:S(2)}) async-start(), calls=%async_computation.20 | async-start | bytes 1966080 | tf_op jit(solution)/shard_map/all_gather | solution.py:55
  599.2 60.0 %reduce-scatter.22.cloned.1.call-start = ((), (), s32[]{:S(2)}) async-start(), calls=%async_computation.21 | async-start | bytes 3932160 | tf_op jit(solution)/shard_map/reduce_scatter | solution.py:63
  620.3 88.9 %all-reduce.7.cloned.1.call-start = ((), (), s32[]{:S(2)}) async-start(), calls=%async_computation.26 | async-start | bytes 1310720
  672.8 50.3 %reduce-scatter.24.cloned.1.call-start = ((), (), s32[]{:S(2)}) async-start(), calls=%async_computation.22 | async-start | bytes 983040 | tf_op jit(solution)/shard_map/reduce_scatter | solution.py:297
  695.8 73.5 %all-gather.24.cloned.1.call-start = ((), (), s32[]{:S(2)}) async-start(), calls=%async_computation.23 | async-start | bytes 4177920 | tf_op jit(solution)/shard_map/all_gather | solution.py:59
  728.3 96.9 %all-gather.16.cloned.1.call-start = ((), (), s32[]{:S(2)}) async-start(), calls=%async_computation.14 | async-start | bytes 5898240 | tf_op jit(solution)/shard_map/all_gather | solution.py:59
  728.9 222.8 %reduce-scatter.26.cloned.1.call-start = ((), (), s32[]{:S(2)}) async-start(), calls=%async_computation.24 | async-start | bytes 1966080 | tf_op jit(solution)/shard_map/reduce_scatter | solution.py:69
  786.3 205.8 %reduce-scatter.16.cloned.1.call-start = ((), (), s32[]{:S(2)}) async-start(), calls=%async_computation.15 | async-start | bytes 1966080 | tf_op jit(solution)/shard_map/reduce_scatter | solution.py:69
  834.5 799.4 %all-reduce.9.cloned.1.call-start = ((), (), s32[]{:S(2)}) async-start(), calls=%async_computation.27 | async-start | bytes 50331648 | tf_op jit(solution)/shard_map/psum | solution.py:348
  874.7 117.4 %copy-start.18 = (bf16[320,1024]{1,0:T(8,128)(2,1)S(1)}, bf16[320,1024]{1,0:T(8,128)(2,1)}, u32[]{:S(2)}) copy-start(bf16[320,1024]{1,0:T(8,128)(2,1)} %reduce-scatter.20.cloned.1.call-done) | copy-start | bytes 1966084
  874.7 117.4 %copy-start.56 = (f32[320]{0:T(512)S(1)}, f32[320]{0:T(512)}, u32[]{:S(2)}) copy-start(f32[320]{0:T(512)} %copy-done.55) | copy-start | bytes 3844
  874.7 117.4 %copy-start.10 = (bf16[320,1024]{1,0:T(8,128)(2,1)S(1)}, bf16[320,1024]{1,0:T(8,128)(2,1)}, u32[]{:S(2)}) copy-start(bf16[320,1024]{1,0:T(8,128)(2,1)} %reduce-scatter.12.cloned.1.call-done) | copy-start | bytes 1966084
  874.8 117.4 %copy-start.17 = (bf16[320,1024]{1,0:T(8,128)(2,1)S(1)}, bf16[320,1024]{1,0:T(8,128)(2,1)}, u32[]{:S(2)}) copy-start(bf16[320,1024]{1,0:T(8,128)(2,1)} %param.29) | copy-start | bytes 1966084
  (66 other events, 592.5 us)
Sparse Core Ops, SparseCore 0:
  17.4 11.2 all-gather.9
  42.7 70.4 reduce-scatter.27
  185.8 24.9 all-gather.11
  220.9 8.7 reduce-scatter.11
  238.3 10.6 all-gather.13
  250.5 10.5 all-gather.17
  266.7 95.2 reduce-scatter.13
  364.9 94.1 reduce-scatter.17
  468.1 98.0 all-gather.19
  580.8 8.7 reduce-scatter.19
  599.4 10.5 all-gather.21
  620.4 38.7 reduce-scatter.21
  673.0 31.4 all-reduce.6
  707.1 15.9 reduce-scatter.23
  728.4 40.8 all-gather.23
  771.4 53.7 all-gather.15
  827.9 8.7 reduce-scatter.25
  839.4 9.9 reduce-scatter.15
  874.9 758.9 all-reduce.8
